TPU v7x, 128 devices: a whole 4x4x4 slice. The times are simulated.
128 devices in a mesh: section: 2 (over y_hi), ctx: 16 (over y_lo, x, core), dp: 4 (over z).
Axes of the slice: x: 4, y: 4 (y_hi: 2, y_lo: 2; y = y_hi * 2 + y_lo), z: 4, core: 2. Of those that a mesh axis runs over, the one named last changes fastest.
Arguments:
- new_input: bfloat16 [2, 4, 2048, 6144], P('section', 'dp', 'ctx'), may hold values from -6 to 6
- new_query: bfloat16 [2, 4, 2048, 6144], P('section', 'dp', 'ctx'), may hold values from -6 to 6
- new_key: bfloat16 [2, 4, 2048, 6144], P('section', 'dp', 'ctx'), may hold values from -6 to 6
- new_value: bfloat16 [2, 4, 2048, 6144], P('section', 'dp', 'ctx'), may hold values from -6 to 6
- new_modality: int32 [2, 4, 2048], P('section', 'dp', 'ctx'), may hold values from 0 to 1, as said below
- old_query: bfloat16 [2, 4, 2048, 6144], P('section', 'dp', 'ctx'), may hold values from -6 to 6
- old_key: bfloat16 [2, 4, 2048, 6144], P('section', 'dp', 'ctx'), may hold values from -6 to 6
- old_value: bfloat16 [2, 4, 2048, 6144], P('section', 'dp', 'ctx'), may hold values from -6 to 6
- old_output: bfloat16 [2, 4, 2048, 6144], P('section', 'dp', 'ctx'), may hold values from -4 to 4
- old_cotangent: bfloat16 [2, 4, 2048, 6144], P('section', 'dp', 'ctx'), may hold values from -6 to 6
- old_modality: int32 [2, 4, 2048], P('section', 'dp', 'ctx'), may hold values from 0 to 1, as said below
- cross_bias: float32 [2, 48], P('section', 'ctx'), may hold values from -2 to 2
Outputs:
- next_input: bfloat16 [2, 4, 2048, 6144], P('section', 'dp', 'ctx')
- query_cotangent: bfloat16 [2, 4, 2048, 6144], P('section', 'dp', 'ctx')
- key_cotangent: bfloat16 [2, 4, 2048, 6144], P('section', 'dp', 'ctx')
- value_cotangent: bfloat16 [2, 4, 2048, 6144], P('section', 'dp', 'ctx')
- bias_cotangent: float32 [2, 48], P('section', 'ctx')
Inputs may be any that keep to these rules, and one draw needn't show every extreme that they name: `new_modality`: 1 marks a trajectory token, 0 a video token. `old_modality`: 1 marks a trajectory token, 0 a video token.
All inputs are finite; a program needn't handle non-finite values.
Results may differ from a plain program's by a relative error of at most 0.0049.
Values may be sent and summed in bfloat16 or wider, within the bound.
A program may use at most 192 MiB of HBM per device.

v0:
```python
import jax
import jax.numpy as jnp
from jax import lax
from jax.sharding import PartitionSpec as P


def from_behind(x, axis, by):
    peers = lax.axis_size(axis)
    return lax.ppermute(x, axis, [(i, (i + by) % peers) for i in range(peers)])


def block_weights(query_block, key_heads, modality_rows, modality_cols, biases, scaling):
    scores = (
        jnp.einsum("hqd,hkd->hqk", query_block, key_heads, preferred_element_type=jnp.float32)
        * scaling
    )
    trajectory_rows = (modality_rows == 1)[:, None]
    video_cols = (modality_cols == 0)[None, :]
    crossing = (trajectory_rows & video_cols).astype(jnp.float32)
    scores = scores + biases[:, None, None] * crossing[None]
    scores = jnp.where((trajectory_rows | video_cols)[None], scores, -jnp.inf)
    highest = jnp.max(scores, axis=2, keepdims=True)
    weights = jnp.exp(scores - highest)
    return (weights / jnp.sum(weights, axis=2, keepdims=True), crossing)


def heads_major(tensor, head_count):
    length = tensor.shape[2]
    split = tensor.reshape(length, head_count, tensor.shape[3] // head_count)
    return jnp.transpose(split, (1, 0, 2))


def tokens_major(stacked_heads):
    head_count, length, head_width = stacked_heads.shape
    return jnp.transpose(stacked_heads, (1, 0, 2)).reshape(1, 1, length, head_count * head_width)


def block_sizes(length):
    block_rows = min(512, length)
    return (block_rows, length // block_rows)


def forward_heads(stacked, modality_all, biases):
    head_count = biases.shape[0]
    query_heads = heads_major(stacked[0], head_count)
    key_heads = heads_major(stacked[1], head_count)
    value_heads = heads_major(stacked[2], head_count)
    length, head_width = (query_heads.shape[1], query_heads.shape[2])
    scaling = head_width ** (-0.5)
    block_rows, block_total = block_sizes(length)

    def forward_one_block(running, offset):
        query_block = lax.dynamic_slice_in_dim(query_heads, offset, block_rows, 1)
        modality_block = lax.dynamic_slice_in_dim(modality_all, offset, block_rows, 0)
        weights, unused = block_weights(
            query_block, key_heads, modality_block, modality_all, biases, scaling
        )
        attended = jnp.einsum(
            "hqk,hkd->hqd",
            weights.astype(jnp.bfloat16),
            value_heads,
            preferred_element_type=jnp.float32,
        )
        return (running, attended.astype(jnp.bfloat16))

    unused, blocks = lax.scan(
        forward_one_block,
        jnp.zeros((), jnp.int32),
        jnp.arange(block_total, dtype=jnp.int32) * block_rows,
    )
    joined = jnp.transpose(blocks, (1, 0, 2, 3)).reshape(head_count, length, head_width)
    return tokens_major(joined)


def backward_heads(stacked, delta_heads, modality_all, biases):
    head_count = biases.shape[0]
    query_heads = heads_major(stacked[0], head_count)
    key_heads = heads_major(stacked[1], head_count)
    value_heads = heads_major(stacked[2], head_count)
    upstream_heads = heads_major(stacked[3], head_count)
    delta_major = jnp.transpose(delta_heads)
    length, head_width = (query_heads.shape[1], query_heads.shape[2])
    scaling = head_width ** (-0.5)
    block_rows, block_total = block_sizes(length)

    def backward_one_block(running, offset):
        key_sum, value_sum, bias_sum = running
        query_block = lax.dynamic_slice_in_dim(query_heads, offset, block_rows, 1)
        upstream_block = lax.dynamic_slice_in_dim(upstream_heads, offset, block_rows, 1)
        delta_block = lax.dynamic_slice_in_dim(delta_major, offset, block_rows, 1)
        modality_block = lax.dynamic_slice_in_dim(modality_all, offset, block_rows, 0)
        weights, crossing = block_weights(
            query_block, key_heads, modality_block, modality_all, biases, scaling
        )
        weights_low = weights.astype(jnp.bfloat16)
        value_sum = value_sum + jnp.einsum(
            "hqk,hqd->hkd", weights_low, upstream_block, preferred_element_type=jnp.float32
        )
        weight_sens = jnp.einsum(
            "hqd,hkd->hqk", upstream_block, value_heads, preferred_element_type=jnp.float32
        )
        score_sens = weights * (weight_sens - delta_block[:, :, None])
        bias_sum = bias_sum + jnp.sum(score_sens * crossing[None], axis=(1, 2))
        rounded = score_sens.astype(jnp.bfloat16)
        query_back = (
            jnp.einsum("hqk,hkd->hqd", rounded, key_heads, preferred_element_type=jnp.float32)
            * scaling
        ).astype(jnp.bfloat16)
        key_sum = key_sum + jnp.einsum(
            "hqk,hqd->hkd", rounded, query_block, preferred_element_type=jnp.float32
        )
        return ((key_sum, value_sum, bias_sum), query_back)

    zeros_heads = jnp.zeros((head_count, length, head_width), jnp.float32)
    initial = (zeros_heads, zeros_heads, jnp.zeros((head_count,), jnp.float32))
    finals, blocks = lax.scan(
        backward_one_block, initial, jnp.arange(block_total, dtype=jnp.int32) * block_rows
    )
    query_joined = jnp.transpose(blocks, (1, 0, 2, 3)).reshape(head_count, length, head_width)
    query_back = tokens_major(query_joined)
    key_back = tokens_major((finals[0] * scaling).astype(jnp.bfloat16))
    value_back = tokens_major(finals[1].astype(jnp.bfloat16))
    return (query_back, key_back, value_back, finals[2])


def shards(
    new_input,
    new_query,
    new_key,
    new_value,
    new_modality,
    old_query,
    old_key,
    old_value,
    old_output,
    old_cotangent,
    old_modality,
    cross_bias,
):
    biases = cross_bias[0]
    head_count = biases.shape[0]
    modality_new, modality_old = (
        lax.all_gather(new_modality, "ctx", axis=2, tiled=True),
        lax.all_gather(old_modality, "ctx", axis=2, tiled=True),
    )
    modality_new = modality_new[0, 0]
    modality_old = modality_old[0, 0]
    exchanged = (
        lax.all_to_all(new_query, "ctx", split_axis=3, concat_axis=2, tiled=True),
        lax.all_to_all(new_key, "ctx", split_axis=3, concat_axis=2, tiled=True),
        lax.all_to_all(new_value, "ctx", split_axis=3, concat_axis=2, tiled=True),
    )
    attended = forward_heads(exchanged, modality_new, biases)
    returned = lax.all_to_all(attended, "ctx", split_axis=2, concat_axis=3, tiled=True)
    summed = (new_input.astype(jnp.float32) + returned.astype(jnp.float32)).astype(jnp.bfloat16)
    next_input = from_behind(summed, "section", 1)
    exchanged = (
        lax.all_to_all(old_query, "ctx", split_axis=3, concat_axis=2, tiled=True),
        lax.all_to_all(old_key, "ctx", split_axis=3, concat_axis=2, tiled=True),
        lax.all_to_all(old_value, "ctx", split_axis=3, concat_axis=2, tiled=True),
        lax.all_to_all(old_cotangent, "ctx", split_axis=3, concat_axis=2, tiled=True),
        lax.all_to_all(old_output, "ctx", split_axis=3, concat_axis=2, tiled=True),
    )
    length = exchanged[3].shape[2]
    width = exchanged[3].shape[3]
    upstream_flat = exchanged[3].reshape(length, head_count, width // head_count)
    output_flat = exchanged[4].reshape(length, head_count, width // head_count)
    delta_heads = jnp.sum(
        upstream_flat.astype(jnp.float32) * output_flat.astype(jnp.float32), axis=2
    )
    query_back, key_back, value_back, bias_local = backward_heads(
        exchanged, delta_heads, modality_old, biases
    )
    returned = (
        lax.all_to_all(query_back, "ctx", split_axis=2, concat_axis=3, tiled=True),
        lax.all_to_all(key_back, "ctx", split_axis=2, concat_axis=3, tiled=True),
        lax.all_to_all(value_back, "ctx", split_axis=2, concat_axis=3, tiled=True),
    )
    bias_total = lax.psum(bias_local[None, :], "dp")
    returned, bias_total = (returned, bias_total)
    return (next_input, returned[0], returned[1], returned[2], bias_total)


def solution(mesh):
    placed = (
        P("section", "dp", "ctx", None),
        P("section", "dp", "ctx", None),
        P("section", "dp", "ctx", None),
        P("section", "dp", "ctx", None),
        P("section", "dp", "ctx"),
        P("section", "dp", "ctx", None),
        P("section", "dp", "ctx", None),
        P("section", "dp", "ctx", None),
        P("section", "dp", "ctx", None),
        P("section", "dp", "ctx", None),
        P("section", "dp", "ctx"),
        P("section", "ctx"),
    )
    return jax.shard_map(
        shards,
        mesh=mesh,
        in_specs=placed,
        out_specs=(
            P("section", "dp", "ctx", None),
            P("section", "dp", "ctx", None),
            P("section", "dp", "ctx", None),
            P("section", "dp", "ctx", None),
            P("section", "ctx"),
        ),
        check_vma=False,
    )
```

profile of v0, /device:TPU:1, one launch (start us, length us, event | category | flops | bytes accessed | tf_op | source)
XLA Modules:
  0.0 1146.8 jit_solution(1504021821421139504)
XLA Ops:
  0.6 6.8 copy.148
  8.0 34.4 %reduce.6 = bf16[6144,128]{1,0:T(8,128)(2,1)} reduce(bf16[6144,1,1,128]{3,2,1,0:T(2,128)(2,1)S(1)} %bitcast.186, bf16[]{:T(256)} %broadcast.170), dimensions={1,2}, to_apply=%bitcast.133.reduce_sub_computation | reduce | bytes 3145730
  46.8 7.5 all-to-all-start.6
  54.3 6.8 copy.152
  61.1 34.4 %reduce.8 = bf16[6144,128]{1,0:T(8,128)(2,1)} reduce(bf16[6144,1,1,128]{3,2,1,0:T(2,128)(2,1)S(1)} %bitcast.204, bf16[]{:T(256)} %broadcast.170), dimensions={1,2}, to_apply=%bitcast.137.reduce_sub_computation | reduce | bytes 3145730
  105.9 6.8 copy.146
  112.8 34.4 %reduce.5 = bf16[6144,128]{1,0:T(8,128)(2,1)} reduce(bf16[6144,1,1,128]{3,2,1,0:T(2,128)(2,1)S(1)} %bitcast.205, bf16[]{:T(256)} %broadcast.170), dimensions={1,2}, to_apply=%bitcast.131.reduce_sub_computation | reduce | bytes 3145730
  157.6 6.8 copy.150
  164.5 34.4 %reduce.7 = bf16[6144,128]{1,0:T(8,128)(2,1)} reduce(bf16[6144,1,1,128]{3,2,1,0:T(2,128)(2,1)S(1)} %bitcast.206, bf16[]{:T(256)} %broadcast.170), dimensions={1,2}, to_apply=%bitcast.135.reduce_sub_computation | reduce | bytes 3145730
  209.4 6.8 copy.144
  216.2 34.4 %reduce.4 = bf16[6144,128]{1,0:T(8,128)(2,1)} reduce(bf16[6144,1,1,128]{3,2,1,0:T(2,128)(2,1)S(1)} %bitcast.207, bf16[]{:T(256)} %broadcast.170), dimensions={1,2}, to_apply=%bitcast.129.reduce_sub_computation | reduce | bytes 3145730
  261.2 6.8 copy.132
  268.0 34.4 %reduce.1 = bf16[6144,128]{1,0:T(8,128)(2,1)} reduce(bf16[6144,1,1,128]{3,2,1,0:T(2,128)(2,1)S(1)} %bitcast.208, bf16[]{:T(256)} %broadcast.170), dimensions={1,2}, to_apply=%bitcast.123.reduce_sub_computation | reduce | bytes 3145730
  306.8 6.4 all-to-all-start.1
  313.2 6.8 copy.134
  320.0 34.4 %reduce.2 = bf16[6144,128]{1,0:T(8,128)(2,1)} reduce(bf16[6144,1,1,128]{3,2,1,0:T(2,128)(2,1)S(1)} %bitcast.209, bf16[]{:T(256)} %broadcast.170), dimensions={1,2}, to_apply=%bitcast.125.reduce_sub_computation | reduce | bytes 3145730
  364.8 6.8 copy.130
  371.7 34.4 %reduce = bf16[6144,128]{1,0:T(8,128)(2,1)} reduce(bf16[6144,1,1,128]{3,2,1,0:T(2,128)(2,1)S(1)} %bitcast.210, bf16[]{:T(256)} %broadcast.170), dimensions={1,2}, to_apply=%bitcast.121.reduce_sub_computation | reduce | bytes 3145730
  416.2 34.1 %all_gather.7 = s32[1,1,2048]{2,1,0:T(1,128)} all-gather(s32[1,1,128]{2,1,0:T(1,128)S(1)} %copy-done.6), channel_id=1, replica_groups=mesh['section'=2,'ctx'=16,'dp'=4] {'ctx'}, dimensions={2}, use_global_device_ids=true | all-gather | bytes 8704 | tf_op jit(solution)/shard_map/all_gather | solution.py:144
  450.4 16.9 %all_gather.6 = s32[1,1,2048]{2,1,0:T(1,128)S(1)} all-gather(s32[1,1,128]{2,1,0:T(1,128)S(1)} %copy-done.7), channel_id=1, replica_groups=mesh['section'=2,'ctx'=16,'dp'=4] {'ctx'}, dimensions={2}, use_global_device_ids=true | all-gather | bytes 8704 | tf_op jit(solution)/shard_map/all_gather | solution.py:143
  467.2 8.3 reshape.224
  478.8 8.1 reshape.228
  494.3 8.1 reshape.222
  506.0 8.1 reshape.226
  517.7 8.1 reshape.220
  529.1 8.1 reshape.214
  540.7 8.1 reshape.216
  552.4 8.1 reshape.212
  564.1 92.6 %while.27 = (s32[]{:T(128)}, bf16[4,3,512,128]{3,2,0,1:T(8,128)(2,1)S(1)}, s32[4]{0:T(128)S(1)}, s32[2048]{0:T(1024)S(1)}, bf16[3,2048,128]{1,2,0:T(8,128)(2,1)}...) while((s32[]{:T(128)}, ...), condition=%wide.region_3.4_spmd, body=%wide.region_0.3_spmd.sunk | while | flops 2460164096 | bytes 21657780 | solution.py:66
  570.0 8.3 fusion.136
  578.3 9.2 fusion.137
  593.0 8.3 fusion.136
  601.3 9.2 fusion.137
  616.0 8.3 fusion.136
  624.3 9.2 fusion.137
  639.0 8.3 fusion.136
  647.3 9.2 fusion.137
  658.3 7.9 copy.141
  666.2 34.4 %reduce.3 = bf16[2048,384]{1,0:T(8,128)(2,1)} reduce(bf16[2048,1,1,384]{3,2,1,0:T(2,128)(2,1)S(1)} %bitcast.197, bf16[]{:T(256)} %broadcast.170), dimensions={1,2}, to_apply=%bitcast.127.reduce_sub_computation | reduce | bytes 3145730
  713.7 192.2 %while.28 = (s32[]{:T(128)}, f32[3,2048,128]{2,1,0:T(8,128)S(1)}, f32[3,2048,128]{2,1,0:T(8,128)}, f32[3]{0:T(128)S(1)}, bf16[4,3,512,128]{3,2,0,1:T(8,128)(2,1)...) while((s32[]{:T(128)}, f32[3,2048,128]{2,1,0:T(8,128)S(1)}, ...), condition=%wide.region_9.10_spmd.clone, body=%wide.region_5.9_spmd.clone.sunk | while | flops 4898299904 | bytes 91542848 | solution.py:116
  720.0 13.1 %fusion.149 = (f32[3,512]{1,0:T(4,128)S(1)}, f32[3,512,2048]{2,1,0:T(8,128)}) fusion(f32[512,2048]{1,0:T(8,128)} %get-tuple-element.453, f32[3]{0:T(128)S(1)} %bitcast.244, pred[512,2048]{1,0:T(8,128)(4,1)} %get-tuple-element.454, bf16[3,2048,128]{2,1,0:T(8,128)(2,1)} %get-tuple-element.532, bf16[3,2048,128]{1,2,0:T(8,128)(2,1)} %get-tuple-element.531, ...), kind=kOutput, calls=%fused_computation.84.clone.1 | convolution fusion | flops 824182784 | bytes 19798032 | tf_op jit(solution)/shard_map/while/body/eval_jaxpr/sub | solution.py:23
  733.1 12.1 %select_add_fusion.5 = f32[3,2048,128]{2,1,0:T(8,128)} fusion(f32[3,2048,128]{2,1,0:T(8,128)} %get-tuple-element.510, f32[3,512]{1,0:T(4,128)S(1)} %get-tuple-element.456, pred[]{:T(512)S(6)} %compare.3, bf16[3,2048,128]{1,2,0:T(8,128)(2,1)} %get-tuple-element.534, s32[]{:T(128)S(6)} %select_n.50, f32[512,2048]{1,0:T(8,128)} %get-tuple-element.453, ...), kind=kOutput, calls=%fused_computation.44.clone.1 | convolution fusion | flops 1634209280 | bytes 13901324 | tf_op jit(solution)/shard_map/while/body/eval_jaxpr/hqk,hqd->hkd/dot_general | solution.py:96
  745.3 8.6 multiply_reduce_fusion.3
  767.2 13.1 %fusion.149 = (f32[3,512]{1,0:T(4,128)S(1)}, f32[3,512,2048]{2,1,0:T(8,128)}) fusion(f32[512,2048]{1,0:T(8,128)} %get-tuple-element.453, f32[3]{0:T(128)S(1)} %bitcast.244, pred[512,2048]{1,0:T(8,128)(4,1)} %get-tuple-element.454, bf16[3,2048,128]{2,1,0:T(8,128)(2,1)} %get-tuple-element.532, bf16[3,2048,128]{1,2,0:T(8,128)(2,1)} %get-tuple-element.531, ...), kind=kOutput, calls=%fused_computation.84.clone.1 | convolution fusion | flops 824182784 | bytes 19798032 | tf_op jit(solution)/shard_map/while/body/eval_jaxpr/sub | solution.py:23
  780.3 13.1 %select_add_fusion.5 = f32[3,2048,128]{2,1,0:T(8,128)} fusion(f32[3,2048,128]{2,1,0:T(8,128)} %get-tuple-element.510, f32[3,512]{1,0:T(4,128)S(1)} %get-tuple-element.456, pred[]{:T(512)S(6)} %compare.3, bf16[3,2048,128]{1,2,0:T(8,128)(2,1)} %get-tuple-element.534, s32[]{:T(128)S(6)} %select_n.50, f32[512,2048]{1,0:T(8,128)} %get-tuple-element.453, ...), kind=kOutput, calls=%fused_computation.44.clone.1 | convolution fusion | flops 1634209280 | bytes 13901324 | tf_op jit(solution)/shard_map/while/body/eval_jaxpr/hqk,hqd->hkd/dot_general | solution.py:96
  793.5 8.6 multiply_reduce_fusion.3
  815.4 13.0 %fusion.149 = (f32[3,512]{1,0:T(4,128)S(1)}, f32[3,512,2048]{2,1,0:T(8,128)}) fusion(f32[512,2048]{1,0:T(8,128)} %get-tuple-element.453, f32[3]{0:T(128)S(1)} %bitcast.244, pred[512,2048]{1,0:T(8,128)(4,1)} %get-tuple-element.454, bf16[3,2048,128]{2,1,0:T(8,128)(2,1)} %get-tuple-element.532, bf16[3,2048,128]{1,2,0:T(8,128)(2,1)} %get-tuple-element.531, ...), kind=kOutput, calls=%fused_computation.84.clone.1 | convolution fusion | flops 824182784 | bytes 19798032 | tf_op jit(solution)/shard_map/while/body/eval_jaxpr/sub | solution.py:23
  828.5 13.1 %select_add_fusion.5 = f32[3,2048,128]{2,1,0:T(8,128)} fusion(f32[3,2048,128]{2,1,0:T(8,128)} %get-tuple-element.510, f32[3,512]{1,0:T(4,128)S(1)} %get-tuple-element.456, pred[]{:T(512)S(6)} %compare.3, bf16[3,2048,128]{1,2,0:T(8,128)(2,1)} %get-tuple-element.534, s32[]{:T(128)S(6)} %select_n.50, f32[512,2048]{1,0:T(8,128)} %get-tuple-element.453, ...), kind=kOutput, calls=%fused_computation.44.clone.1 | convolution fusion | flops 1634209280 | bytes 13901324 | tf_op jit(solution)/shard_map/while/body/eval_jaxpr/hqk,hqd->hkd/dot_general | solution.py:96
  841.7 8.6 multiply_reduce_fusion.3
  863.6 13.0 %fusion.149 = (f32[3,512]{1,0:T(4,128)S(1)}, f32[3,512,2048]{2,1,0:T(8,128)}) fusion(f32[512,2048]{1,0:T(8,128)} %get-tuple-element.453, f32[3]{0:T(128)S(1)} %bitcast.244, pred[512,2048]{1,0:T(8,128)(4,1)} %get-tuple-element.454, bf16[3,2048,128]{2,1,0:T(8,128)(2,1)} %get-tuple-element.532, bf16[3,2048,128]{1,2,0:T(8,128)(2,1)} %get-tuple-element.531, ...), kind=kOutput, calls=%fused_computation.84.clone.1 | convolution fusion | flops 824182784 | bytes 19798032 | tf_op jit(solution)/shard_map/while/body/eval_jaxpr/sub | solution.py:23
  876.6 13.1 %select_add_fusion.5 = f32[3,2048,128]{2,1,0:T(8,128)} fusion(f32[3,2048,128]{2,1,0:T(8,128)} %get-tuple-element.510, f32[3,512]{1,0:T(4,128)S(1)} %get-tuple-element.456, pred[]{:T(512)S(6)} %compare.3, bf16[3,2048,128]{1,2,0:T(8,128)(2,1)} %get-tuple-element.534, s32[]{:T(128)S(6)} %select_n.50, f32[512,2048]{1,0:T(8,128)} %get-tuple-element.453, ...), kind=kOutput, calls=%fused_computation.44.clone.1 | convolution fusion | flops 1634209280 | bytes 13901324 | tf_op jit(solution)/shard_map/while/body/eval_jaxpr/hqk,hqd->hkd/dot_general | solution.py:96
  889.8 8.6 multiply_reduce_fusion.3
  911.6 7.9 copy.163
  919.5 34.4 %reduce.10 = bf16[2048,384]{1,0:T(8,128)(2,1)} reduce(bf16[2048,1,1,384]{3,2,1,0:T(2,128)(2,1)S(1)} %bitcast.198, bf16[]{:T(256)} %broadcast.170), dimensions={1,2}, to_apply=%bitcast.141.reduce_sub_computation | reduce | bytes 3145730
  958.4 6.3 all-to-all-start.10
  967.9 7.9 copy.160
  975.8 34.4 %reduce.9 = bf16[2048,384]{1,0:T(8,128)(2,1)} reduce(bf16[2048,1,1,384]{3,2,1,0:T(2,128)(2,1)S(1)} %bitcast.199, bf16[]{:T(256)} %broadcast.170), dimensions={1,2}, to_apply=%bitcast.139.reduce_sub_computation | reduce | bytes 3145730
  1014.6 8.1 reshape.218
  1042.2 7.9 copy.166
  1050.1 34.4 %reduce.11 = bf16[2048,384]{1,0:T(8,128)(2,1)} reduce(bf16[2048,1,1,384]{3,2,1,0:T(2,128)(2,1)S(1)} %bitcast.187, bf16[]{:T(256)} %broadcast.170), dimensions={1,2}, to_apply=%bitcast.143.reduce_sub_computation | reduce | bytes 3145730
  1094.4 10.6 psum.7
  1105.0 8.1 reshape.232
  1118.0 8.1 reshape.230
  1131.0 8.1 reshape.234
  (163 shorter events, 242.3 us)
Async XLA Ops:
  46.8 53.1 %all-to-all-start.6 = ((bf16[16,2,24576]{2,1,0:T(2,128)(2,1)}), bf16[16,2,24576]{2,1,0:T(2,128)(2,1)}, u32[]{:S(2)}, u32[]{:S(2)}) async-start(bf16[16,2,24576]{2,1,0:T(2,128)(2,1)} %reshape.223), calls=%async_computation.6 | async-start | bytes 3145728 | tf_op jit(solution)/shard_map/all_to_all | solution.py:161
  99.9 51.7 %all-to-all-start.8 = ((bf16[16,2,24576]{2,1,0:T(2,128)(2,1)}), bf16[16,2,24576]{2,1,0:T(2,128)(2,1)}, u32[]{:S(2)}, u32[]{:S(2)}) async-start(bf16[16,2,24576]{2,1,0:T(2,128)(2,1)} %reshape.227), calls=%async_computation.8 | async-start | bytes 3145728 | tf_op jit(solution)/shard_map/all_to_all | solution.py:162
  151.6 51.7 %all-to-all-start.5 = ((bf16[16,2,24576]{2,1,0:T(2,128)(2,1)}), bf16[16,2,24576]{2,1,0:T(2,128)(2,1)}, u32[]{:S(2)}, u32[]{:S(2)}) async-start(bf16[16,2,24576]{2,1,0:T(2,128)(2,1)} %reshape.221), calls=%async_computation.5 | async-start | bytes 3145728 | tf_op jit(solution)/shard_map/all_to_all | solution.py:159
  203.3 51.7 %all-to-all-start.7 = ((bf16[16,2,24576]{2,1,0:T(2,128)(2,1)}), bf16[16,2,24576]{2,1,0:T(2,128)(2,1)}, u32[]{:S(2)}, u32[]{:S(2)}) async-start(bf16[16,2,24576]{2,1,0:T(2,128)(2,1)} %reshape.225), calls=%async_computation.7 | async-start | bytes 3145728 | tf_op jit(solution)/shard_map/all_to_all | solution.py:160
  255.0 51.8 %all-to-all-start.4 = ((bf16[16,2,24576]{2,1,0:T(2,128)(2,1)}), bf16[16,2,24576]{2,1,0:T(2,128)(2,1)}, u32[]{:S(2)}, u32[]{:S(2)}) async-start(bf16[16,2,24576]{2,1,0:T(2,128)(2,1)} %reshape.219), calls=%async_computation.4 | async-start | bytes 3145728 | tf_op jit(solution)/shard_map/all_to_all | solution.py:158
  306.8 52.0 %all-to-all-start.1 = ((bf16[16,2,24576]{2,1,0:T(2,128)(2,1)}), bf16[16,2,24576]{2,1,0:T(2,128)(2,1)}, u32[]{:S(2)}, u32[]{:S(2)}) async-start(bf16[16,2,24576]{2,1,0:T(2,128)(2,1)} %reshape.213), calls=%async_computation.1 | async-start | bytes 3145728 | tf_op jit(solution)/shard_map/all_to_all | solution.py:150
  358.8 51.7 %all-to-all-start.2 = ((bf16[16,2,24576]{2,1,0:T(2,128)(2,1)}), bf16[16,2,24576]{2,1,0:T(2,128)(2,1)}, u32[]{:S(2)}, u32[]{:S(2)}) async-start(bf16[16,2,24576]{2,1,0:T(2,128)(2,1)} %reshape.215), calls=%async_computation.2 | async-start | bytes 3145728 | tf_op jit(solution)/shard_map/all_to_all | solution.py:151
  406.1 10.2 copy-start.6
  406.1 44.3 %copy-start.7 = (s32[1,1,128]{2,1,0:T(1,128)S(1)}, s32[1,1,128]{2,1,0:T(1,128)}, u32[]{:S(2)}) copy-start(s32[1,1,128]{2,1,0:T(1,128)} %param.20) | copy-start | bytes 1540
  410.5 141.9 %all-to-all-start = ((bf16[16,2,24576]{2,1,0:T(2,128)(2,1)}), bf16[16,2,24576]{2,1,0:T(2,128)(2,1)}, u32[]{:S(2)}, u32[]{:S(2)}) async-start(bf16[16,2,24576]{2,1,0:T(2,128)(2,1)} %reshape.211), calls=%async_computation | async-start | bytes 3145728 | tf_op jit(solution)/shard_map/all_to_all | solution.py:149
  561.7 2.3 copy-start.8
  705.0 253.5 %all-to-all-start.3 = ((bf16[16,2,24576]{2,1,0:T(2,128)(2,1)}), bf16[16,2,24576]{2,1,0:T(2,128)(2,1)}, u32[]{:S(2)}, u32[]{:S(2)}) async-start(bf16[16,2,24576]{2,1,0:T(2,128)(2,1)} %reshape.217), calls=%async_computation.3 | async-start | bytes 3145728 | tf_op jit(solution)/shard_map/all_to_all | solution.py:154
  709.3 4.4 copy-start
  709.3 4.4 copy-start.4
  709.3 4.4 copy-start.5
  753.9 4.9 copy-start.3
  802.1 4.9 copy-start.3
  850.3 4.9 copy-start.3
  898.3 4.8 copy-start.3
  953.9 10.8 copy-start.2
  958.4 7.9 copy-start.1
  958.4 68.9 %all-to-all-start.10 = ((bf16[16,2,24576]{2,1,0:T(2,128)(2,1)}), bf16[16,2,24576]{2,1,0:T(2,128)(2,1)}, u32[]{:S(2)}, u32[]{:S(2)}) async-start(bf16[16,2,24576]{2,1,0:T(2,128)(2,1)} %reshape.231), calls=%async_computation.10 | async-start | bytes 3145728 | tf_op jit(solution)/shard_map/all_to_all | solution.py:176
  1027.3 61.6 %all-to-all-start.9 = ((bf16[16,2,24576]{2,1,0:T(2,128)(2,1)}), bf16[16,2,24576]{2,1,0:T(2,128)(2,1)}, u32[]{:S(2)}, u32[]{:S(2)}) async-start(bf16[16,2,24576]{2,1,0:T(2,128)(2,1)} %reshape.229), calls=%async_computation.9 | async-start | bytes 3145728 | tf_op jit(solution)/shard_map/all_to_all | solution.py:175
  1036.3 107.7 %collective-permute-start = (bf16[1,1,128,6144]{2,3,1,0:T(8,128)(2,1)}, bf16[1,1,128,6144]{2,3,1,0:T(8,128)(2,1)}, u32[]{:S(2)}, u32[]{:S(2)}) collective-permute-start(bf16[1,1,128,6144]{2,3,1,0:T(8,128)(2,1)} %fusion.94), channel_id=1, source_target_pairs={{0,64},{64,0},{1,65},{65,1},{2,66},{66,2},{3,67},{67,3},{4,68},{68... | collective-permute-start | bytes 4718600 | tf_op jit(solution)/shard_map/ppermute | solution.py:9
  1089.0 42.0 %all-to-all-start.11 = ((bf16[16,2,24576]{2,1,0:T(2,128)(2,1)}), bf16[16,2,24576]{2,1,0:T(2,128)(2,1)}, u32[]{:S(2)}, u32[]{:S(2)}) async-start(bf16[16,2,24576]{2,1,0:T(2,128)(2,1)} %reshape.233), calls=%async_computation.11 | async-start | bytes 3145728 | tf_op jit(solution)/shard_map/all_to_all | solution.py:177
where the time goes:
time: 1160 us; the launch traced here: 1150 us
  other arithmetic  453 us (39%)
  local copies, waits for them, and re-layouts  302 us (26%)
  matrix products  238 us (21%)
  starting transfers between devices  74.3 us (6%)
  blocking collectives  61.6 us (5%)
  loops' own time  16.9 us (1%)
    unnamed x15, other arithmetic  413 us
    unnamed x66, local copies, waits for them, and re-layouts  223 us
    sub x8, matrix products, block_weights(): weights = jnp.exp(scores - highest)  85.4 us
    dot_general x4, matrix products, backward_one_block(): jnp.einsum('hqk,hqd->hkd', weights_low, upstream_block, preferred_element...  51.5 us
    dot_general x4, matrix products, forward_one_block(): jnp.einsum('hqk,hkd->hqd', weights.astype(jnp.bfloat16), value_heads, pre...  36.9 us
    dot_general x4, matrix products, backward_one_block(): jnp.einsum('hqd,hkd->hqk', upstream_block, value_heads, preferred_element...  34.3 us
    all_gather x1, blocking collectives, shards(): lax.all_gather(old_modality, 'ctx', axis=2, tiled=True)  34.1 us
    reshape x4, local copies, waits for them, and re-layouts, tokens_major(): jnp.transpose(stacked_heads, (1, 0, 2))  31.7 us
  transfers between devices with their start and end apart: 13, of which 0 were waited for; matrix products, arithmetic and copies ran while one was open for 70% of the time, Pallas kernels for 0%

commit v1 on v0

v1 whole, which is shorter than its diff:
```python
import functools

import jax
import jax.numpy as jnp
from jax import lax
from jax.experimental import pallas as pl
from jax.experimental.pallas import tpu as pltpu
from jax.sharding import PartitionSpec as P

MESH = pl.DeviceIdType.MESH
NT = (((1,), (1,)), ((), ()))
TN = (((0,), (0,)), ((), ()))
F32 = jnp.float32
BF16 = jnp.bfloat16
NEG = -1e30
LOG2E = 1.4426950408889634
LANES = 128


def forward_block(i, bq, q_ref, k_ref, v_ref, o_ref, row_ref, col_ref, bias):
    length, width = k_ref.shape
    c1 = width**-0.5 * LOG2E
    rows = pl.ds(pl.multiple_of(i * bq, bq), bq)
    scores = lax.dot_general(q_ref[rows, :], k_ref[...], NT, preferred_element_type=F32)
    traj = col_ref[rows, :] > 0.5
    logits, top = [], None
    for c in range(length // LANES):
        cols = slice(c * LANES, (c + 1) * LANES)
        key_traj = row_ref[:, cols]
        yes = (1.0 - key_traj) * (bias * LOG2E)
        no = key_traj * NEG
        x = scores[:, cols] * c1 + jnp.where(traj, yes, no)
        logits.append(x)
        top = x if top is None else jnp.maximum(top, x)
    top = jnp.max(top, axis=1, keepdims=True)
    total, weights = None, []
    for x in logits:
        p = jnp.exp2(x - top)
        total = p if total is None else total + p
        weights.append(p.astype(BF16))
    total = jnp.sum(total, axis=1, keepdims=True)
    out = jnp.dot(jnp.concatenate(weights, axis=1), v_ref[...], preferred_element_type=F32)
    o_ref[rows, :] = (out / total).astype(BF16)


def backward_block(
    i, bq, bk, q_ref, k_ref, v_ref, do_ref, dq_ref, dk_acc, dv_acc, x_scr, ds_scr, b_acc, row_ref, col_ref, del_ref, bias
):
    length, width = k_ref.shape
    scale = width**-0.5
    c1 = scale * LOG2E
    rows = pl.ds(pl.multiple_of(i * bq, bq), bq)
    q = q_ref[rows, :]
    do = do_ref[rows, :]
    traj = row_ref[:, rows]
    yes = traj * (bias * LOG2E)
    no = (1.0 - traj) * NEG
    delta = del_ref[:, rows]
    blocks = [slice(c * bk, (c + 1) * bk) for c in range(length // bk)]

    def video(ks):
        return jnp.concatenate([col_ref[ks, :]] * (bq // LANES), axis=1) < 0.5

    def fold(x):
        return x.reshape(bk // 8, 8, bq)

    top = None
    for ks in blocks:
        s = lax.dot_general(k_ref[ks, :], q, NT, preferred_element_type=F32)
        x = s * c1 + jnp.where(video(ks), yes, no)
        x_scr[ks, :] = x
        t = jnp.max(fold(x), axis=0)
        top = t if top is None else jnp.maximum(top, t)
    top = jnp.max(top, axis=0, keepdims=True)
    total = None
    for ks in blocks:
        p = jnp.exp2(x_scr[ks, :] - top)
        x_scr[ks, :] = p
        t = jnp.sum(fold(p), axis=0)
        total = t if total is None else total + t
    inverse = 1.0 / jnp.sum(total, axis=0, keepdims=True)
    b_sum = None
    for ks in blocks:
        dp = lax.dot_general(v_ref[ks, :], do, NT, preferred_element_type=F32)
        p = x_scr[ks, :] * inverse
        ds = p * (dp - delta)
        t = jnp.sum(fold(jnp.where(video(ks), ds, 0.0)), axis=0)
        b_sum = t if b_sum is None else b_sum + t
        low = ds.astype(BF16)
        ds_scr[ks, :] = low
        dv_acc[ks, :] += jnp.dot(p.astype(BF16), do, preferred_element_type=F32)
        dk_acc[ks, :] += jnp.dot(low, q, preferred_element_type=F32)
    b_acc[...] += b_sum * traj
    dq = lax.dot_general(ds_scr[...], k_ref[...], TN, preferred_element_type=F32)
    dq_ref[rows, :] = (dq * scale).astype(BF16)


def body(
    heads, bqf, bq, bk,
    ni, nq, nk, nv, oq, ok, ov, oo, oc, nm, om, bias,
    att_out, ni_out, dq_out, dk_out, dv_out, db_out,
    new_buf, old_buf, att, grads, dk_acc, dv_acc, x_scr, ds_scr, b_acc, b_row, db_s, db_r,
    mod_n, mod_o, row_n, row_o, col_n, col_o, c_buf, o_buf, del_s, del_r, del_rows,
    in_recv, in_send, att_recv, att_send, ni_recv, ni_send, g_recv, g_send,
    mod_recv, mod_send, del_recv, del_send, db_recv, db_send, loc_sem,
):
    peers = lax.axis_size("ctx")
    sections = lax.axis_size("section")
    replicas = lax.axis_size("dp")
    me = lax.axis_index("ctx")
    section = lax.axis_index("section")
    replica = lax.axis_index("dp")
    next_section = (section + 1) % sections
    tokens = nq.shape[0]
    width = new_buf.shape[3]
    length = new_buf.shape[2]
    my_rows = pl.ds(pl.multiple_of(me * tokens, tokens), tokens)
    whole = pl.ds(0, (peers - 1) * tokens)

    def head_cols(p, h):
        return pl.ds(pl.multiple_of((p * heads + h) * width, width), width)

    def token_rows(p):
        return pl.ds(pl.multiple_of(p * tokens, tokens), tokens)

    barrier = pltpu.get_barrier_semaphore()

    @pl.loop(1, peers)
    def _(k):
        pl.semaphore_signal(barrier, inc=1, device_id={"ctx": (me + k) % peers}, device_id_type=MESH)

    @pl.loop(0, peers)
    def _(k):
        pl.semaphore_signal(barrier, inc=1, device_id={"section": next_section, "ctx": k}, device_id_type=MESH)

    @pl.loop(1, replicas)
    def _(k):
        pl.semaphore_signal(barrier, inc=1, device_id={"dp": (replica + k) % replicas}, device_id_type=MESH)

    pl.semaphore_wait(barrier, 2 * peers - 1 + replicas - 1)

    load_c = pltpu.make_async_copy(oc, c_buf, loc_sem.at[0])
    load_o = pltpu.make_async_copy(oo, o_buf, loc_sem.at[1])
    for ref, buf, j in ((nm, mod_n, 0), (om, mod_o, 1)):
        pltpu.make_async_copy(ref, buf.at[me], mod_recv.at[j]).start()

        @pl.loop(1, peers)
        def _(k):
            pltpu.make_async_remote_copy(
                src_ref=ref, dst_ref=buf.at[me], send_sem=mod_send.at[j], recv_sem=mod_recv.at[j],
                device_id={"ctx": (me + k) % peers}, device_id_type=MESH,
            ).start()

    def send_in(arrays, buf, first):
        @pl.loop(0, heads)
        def _(h):
            for a, src in enumerate(arrays):
                pltpu.make_async_copy(
                    src.at[:, head_cols(me, h)], buf.at[a, h, my_rows, :], in_recv.at[first + a, h]
                ).start()

            @pl.loop(1, peers)
            def _(k):
                t = (me + k) % peers
                for a, src in enumerate(arrays):
                    pltpu.make_async_remote_copy(
                        src_ref=src.at[:, head_cols(t, h)], dst_ref=buf.at[a, h, my_rows, :],
                        send_sem=in_send.at[first + a, h], recv_sem=in_recv.at[first + a, h],
                        device_id={"ctx": t}, device_id_type=MESH,
                    ).start()

    send_in((nq, nk, nv), new_buf, 0)
    load_c.start()
    load_o.start()
    send_in((oq, ok, ov, oc), old_buf, 3)
    ni_copy = pltpu.make_async_remote_copy(
        src_ref=ni, dst_ref=ni_out, send_sem=ni_send, recv_sem=ni_recv,
        device_id={"section": next_section}, device_id_type=MESH,
    )
    ni_copy.start()

    load_c.wait()
    load_o.wait()

    @pl.loop(0, peers)
    def _(p):
        for j in range(heads):
            cols = head_cols(p, j)
            prod = c_buf[:, cols].astype(F32) * o_buf[:, cols].astype(F32)
            del_s[p, j : j + 1, :] = jnp.sum(prod.T, axis=0, keepdims=True)

    for buf, row, col, j in ((mod_n, row_n, col_n, 0), (mod_o, row_o, col_o, 1)):
        pltpu.make_async_copy(buf, buf, mod_recv.at[j]).wait()
        for c in range(peers):
            flags = (buf[c] == 1).astype(F32)
            row[:, c * tokens : (c + 1) * tokens] = flags
            col[c * tokens : (c + 1) * tokens, :] = jnp.broadcast_to(flags, (LANES, tokens)).T

    def wait_in(buf, a, first, h):
        pltpu.make_async_copy(buf.at[a, h], buf.at[a, h], in_recv.at[first + a, h]).wait()

    @pl.loop(0, heads)
    def _(h):
        for a in range(3):
            wait_in(new_buf, a, 0, h)
        limit = bias[0, h]

        @pl.loop(0, length // bqf)
        def _(i):
            forward_block(
                i, bqf, new_buf.at[0, h], new_buf.at[1, h], new_buf.at[2, h], att.at[h], row_n, col_n, limit
            )

        @pl.loop(0, peers)
        def _(k):
            t = (me + k) % peers
            pltpu.make_async_remote_copy(
                src_ref=att.at[h, token_rows(t), :], dst_ref=att_out.at[:, head_cols(me, h)],
                send_sem=att_send.at[h], recv_sem=att_recv,
                device_id={"section": next_section, "ctx": t}, device_id_type=MESH,
            ).start()

        @pl.when(h == 0)
        def _():
            pltpu.make_async_copy(del_s.at[me], del_r.at[me], del_recv).start()

            @pl.loop(1, peers)
            def _(k):
                t = (me + k) % peers
                pltpu.make_async_remote_copy(
                    src_ref=del_s.at[t], dst_ref=del_r.at[me], send_sem=del_send, recv_sem=del_recv,
                    device_id={"ctx": t}, device_id_type=MESH,
                ).start()

    pltpu.make_async_copy(del_r, del_r, del_recv).wait()
    for c in range(peers):
        for j in range(heads):
            del_rows[j, :, c * tokens : (c + 1) * tokens] = del_r[c, j : j + 1, :]

    b_row[...] = jnp.zeros_like(b_row)
    lane = lax.broadcasted_iota(jnp.int32, (8, LANES), 1)

    @pl.loop(0, heads)
    def _(h):
        for a in range(4):
            wait_in(old_buf, a, 3, h)
        limit = bias[0, h]
        dk_acc[...] = jnp.zeros_like(dk_acc)
        dv_acc[...] = jnp.zeros_like(dv_acc)
        b_acc[...] = jnp.zeros_like(b_acc)

        @pl.loop(0, length // bq)
        def _(i):
            backward_block(
                i, bq, bk, old_buf.at[0, h], old_buf.at[1, h], old_buf.at[2, h], old_buf.at[3, h],
                grads.at[0, h], dk_acc, dv_acc, x_scr, ds_scr, b_acc, row_o, col_o, del_rows.at[h], limit,
            )

        grads[1, h] = (dk_acc[...] * width**-0.5).astype(BF16)
        grads[2, h] = dv_acc[...].astype(BF16)
        share = jnp.sum(jnp.sum(b_acc[...], axis=0, keepdims=True), axis=1, keepdims=True)
        b_row[...] += jnp.where(lane == h, share, 0.0)
        for g, out in enumerate((dq_out, dk_out, dv_out)):
            pltpu.make_async_copy(grads.at[g, h, my_rows, :], out.at[:, head_cols(me, h)], g_recv.at[g]).start()

        @pl.loop(1, peers)
        def _(k):
            t = (me + k) % peers
            for g, out in enumerate((dq_out, dk_out, dv_out)):
                pltpu.make_async_remote_copy(
                    src_ref=grads.at[g, h, token_rows(t), :], dst_ref=out.at[:, head_cols(me, h)],
                    send_sem=g_send.at[g, h], recv_sem=g_recv.at[g],
                    device_id={"ctx": t}, device_id_type=MESH,
                ).start()

    db_s[...] = b_row[...]
    pltpu.make_async_copy(db_s, db_r.at[replica], db_recv).start()

    @pl.loop(1, replicas)
    def _(k):
        pltpu.make_async_remote_copy(
            src_ref=db_s, dst_ref=db_r.at[replica], send_sem=db_send, recv_sem=db_recv,
            device_id={"dp": (replica + k) % replicas}, device_id_type=MESH,
        ).start()

    pltpu.make_async_copy(db_r, db_r, db_recv).wait()
    acc = db_r[0]
    for r in range(1, replicas):
        acc = acc + db_r[r]
    db_out[...] = acc

    def drain(ref, sem):
        pltpu.make_async_copy(ref, ref, sem).wait()

    for j, buf in enumerate((mod_n, mod_o)):
        drain(buf.at[pl.ds(0, peers - 1)], mod_send.at[j])
    drain(del_s.at[pl.ds(0, peers - 1)], del_send)
    drain(db_r.at[pl.ds(0, replicas - 1)], db_send)

    @pl.loop(0, heads)
    def _(h):
        for a in range(3):
            drain(new_buf.at[a, h, whole, :], in_send.at[a, h])
        for a in range(4):
            drain(old_buf.at[a, h, whole, :], in_send.at[3 + a, h])
        drain(att.at[h], att_send.at[h])
        for g in range(3):
            drain(grads.at[g, h, whole, :], g_send.at[g, h])

    ni_copy.wait()
    drain(att_out, att_recv)
    for g, out in enumerate((dq_out, dk_out, dv_out)):
        drain(out, g_recv.at[g])


def shards(
    new_input, new_query, new_key, new_value, new_modality,
    old_query, old_key, old_value, old_output, old_cotangent, old_modality, cross_bias,
):
    tokens, features = new_query.shape[2:]
    heads = cross_bias.shape[1]
    peers = lax.axis_size("ctx")
    replicas = lax.axis_size("dp")
    length = tokens * peers
    width = features // (heads * peers)
    bqf, bq, bk = 256, 256, 256

    def flat(x):
        return x.reshape(x.shape[-2:])

    full = jax.ShapeDtypeStruct((tokens, features), BF16)
    dma = pltpu.SemaphoreType.DMA
    any_spec = pl.BlockSpec(memory_space=pl.ANY)
    att, shifted, dq, dk, dv, db = pl.pallas_call(
        functools.partial(body, heads, bqf, bq, bk),
        out_shape=[full] * 5 + [jax.ShapeDtypeStruct((8, LANES), F32)],
        in_specs=[any_spec] * 11 + [pl.BlockSpec(memory_space=pltpu.SMEM)],
        out_specs=[any_spec] * 5 + [pl.BlockSpec(memory_space=pltpu.VMEM)],
        scratch_shapes=[
            pltpu.VMEM((3, heads, length, width), BF16),
            pltpu.VMEM((4, heads, length, width), BF16),
            pltpu.VMEM((heads, length, width), BF16),
            pltpu.VMEM((3, heads, length, width), BF16),
            pltpu.VMEM((length, width), F32),
            pltpu.VMEM((length, width), F32),
            pltpu.VMEM((length, bq), F32),
            pltpu.VMEM((length, bq), BF16),
            pltpu.VMEM((8, bq), F32),
            pltpu.VMEM((8, LANES), F32),
            pltpu.VMEM((8, LANES), F32),
            pltpu.VMEM((replicas, 8, LANES), F32),
            pltpu.VMEM((peers, 1, tokens), jnp.int32),
            pltpu.VMEM((peers, 1, tokens), jnp.int32),
            pltpu.VMEM((1, length), F32),
            pltpu.VMEM((1, length), F32),
            pltpu.VMEM((length, LANES), F32),
            pltpu.VMEM((length, LANES), F32),
            pltpu.VMEM((tokens, features), BF16),
            pltpu.VMEM((tokens, features), BF16),
            pltpu.VMEM((peers, 8, tokens), F32),
            pltpu.VMEM((peers, 8, tokens), F32),
            pltpu.VMEM((heads, 1, length), F32),
            dma((7, heads)), dma((7, heads)),
            dma, dma((heads,)),
            dma, dma,
            dma((3,)), dma((3, heads)),
            dma((2,)), dma((2,)),
            dma, dma,
            dma, dma,
            dma((2,)),
        ],
        compiler_params=pltpu.CompilerParams(
            collective_id=0, has_side_effects=True, vmem_limit_bytes=62 << 20
        ),
    )(
        flat(new_input), flat(new_query), flat(new_key), flat(new_value),
        flat(old_query), flat(old_key), flat(old_value), flat(old_output), flat(old_cotangent),
        new_modality.reshape(1, tokens), old_modality.reshape(1, tokens), cross_bias,
    )
    summed = (shifted.astype(F32) + att.astype(F32)).astype(BF16)

    def whole(x):
        return x[None, None]

    return whole(summed), whole(dq), whole(dk), whole(dv), db[:1, :heads]


def solution(mesh):
    tokens = P("section", "dp", "ctx", None)
    flags = P("section", "dp", "ctx")
    biases = P("section", "ctx")
    return jax.shard_map(
        shards,
        mesh=mesh,
        in_specs=(tokens,) * 4 + (flags,) + (tokens,) * 5 + (flags, biases),
        out_specs=(tokens,) * 4 + (biases,),
        check_vma=False,
    )
```

time: 1160 us -> 286 us (0.25); the launches traced: 1150 us -> 286 us
  other arithmetic: 453 us -> 3.52 us
  local copies, waits for them, and re-layouts: 302 us -> 6.29 us
  Pallas kernels: 0 us -> 275 us
  matrix products: 238 us -> 0 us
  starting transfers between devices: 74.3 us -> 0 us
  blocking collectives: 61.6 us -> 0 us
  loops' own time: 16.9 us -> 0 us
    unnamed x15 -> x0, other arithmetic: 413 us -> none
    pallas_call x0 -> x1, Pallas kernels: none -> 275 us  [shards(): pl.pallas_call(functools.partial(body, heads, bqf, bq, bk), out_shape=[fu...]
    unnamed x66 -> x9, local copies, waits for them, and re-layouts: 223 us -> 5.1 us
    dot_general x20 -> x0, matrix products: 152 us -> none  [the longest x4 51.5 us: backward_one_block(): jnp.einsum('hqk,hqd->hkd', weights_low, upstream_block, preferred_element...]
    sub x8 -> x0, matrix products: 85.4 us -> none  [block_weights(): weights = jnp.exp(scores - highest)]
    all_to_all x12 -> x0, starting transfers between devices: 71.7 us -> none  [the longest x1 7.48 us: shards(): lax.all_to_all(old_cotangent, 'ctx', split_axis=3, concat_axis=2, tiled=T...]
    all_gather x2 -> x0, blocking collectives: 51 us -> none  [the longest x1 34.1 us: shards(): lax.all_gather(old_modality, 'ctx', axis=2, tiled=True)]
    reshape x11 -> x0, local copies, waits for them, and re-layouts: 40.8 us -> none  [the longest x4 31.7 us: tokens_major(): jnp.transpose(stacked_heads, (1, 0, 2))]
  transfers between devices with their start and end apart: 13 -> 0, of which waited for: 0 -> 0; matrix products, arithmetic and copies ran while one was open for 70% -> 0% of each run, Pallas kernels for 0% -> 0%
where the time goes in v1:
time: 286 us
  Pallas kernels  275 us (96%)
  local copies, waits for them, and re-layouts  6.29 us (2%)
  other arithmetic  3.52 us (1%)
    pallas_call x1, Pallas kernels, shards(): pl.pallas_call(functools.partial(body, heads, bqf, bq, bk), out_shape=[fu...  275 us

profile of v1, /device:TPU:1, one launch (start us, length us, event | category | flops | bytes accessed | tf_op | source)
XLA Modules:
  0.0 285.8 jit_solution(10061562255827013335)
XLA Ops:
  0.6 275.4 %shard_map.155 = (bf16[128,6144]{1,0:T(8,128)(2,1)}, bf16[128,6144]{1,0:T(8,128)(2,1)}, bf16[128,6144]{1,0:T(8,128)(2,1)}, bf16[128,6144]{1,0:T(8,128)(2,1)}, bf...) custom-call(bf16[128,6144]{1,0:T(8,128)(2,1)} %bitcast.19, bf16[128,6144]{1,0:T(8,128)(2,1)} %bitcast.20, ...), custom_call_target="tpu_custom_call" | custom-call | tf_op jit(solution)/shard_map/pallas_call | solution.py:334
  276.0 0.0 copy-start.2
  276.0 3.5 %fusion = bf16[1,1,128,6144]{3,2,1,0:T(8,128)(2,1)} fusion(bf16[128,6144]{1,0:T(8,128)(2,1)} %get-tuple-element.12, bf16[128,6144]{1,0:T(8,128)(2,1)} %get-tuple-element.11), kind=kLoop, calls=%fused_computation.1 | loop fusion | flops 3145728 | bytes 4718592 | tf_op jit(solution)/shard_map/broadcast_in_dim | solution.py:383
  279.5 1.2 slice.3
  280.7 0.0 copy-done.2
  280.7 0.0 copy-start.1
  280.7 1.1 copy.20
  281.9 0.8 copy-done.1
  282.7 0.0 copy-start
  282.7 1.1 copy.21
  283.9 0.8 copy-done
  284.7 1.1 copy.22
Async XLA Ops:
  276.0 4.7 %copy-start.2 = (bf16[128,6144]{1,0:T(8,128)(2,1)S(1)}, bf16[128,6144]{1,0:T(8,128)(2,1)}, u32[]{:S(2)}) copy-start(bf16[128,6144]{1,0:T(8,128)(2,1)} %get-tuple-element.13) | copy-start | bytes 4718596
  280.7 2.0 copy-start.1
  282.7 2.0 copy-start

commit v2 on v1

--- a/solution.py
+++ b/solution.py
@@ -98,10 +98,10 @@
 def body(
     heads, bqf, bq, bk,
     ni, nq, nk, nv, oq, ok, ov, oo, oc, nm, om, bias,
-    att_out, ni_out, dq_out, dk_out, dv_out, db_out,
-    new_buf, old_buf, att, grads, dk_acc, dv_acc, x_scr, ds_scr, b_acc, b_row, db_s, db_r,
+    next_out, dq_out, dk_out, dv_out, db_out,
+    new_buf, old_buf, ni_buf, att, grads, dk_acc, dv_acc, x_scr, ds_scr, b_acc, b_row, db_s, db_r,
     mod_n, mod_o, row_n, row_o, col_n, col_o, c_buf, o_buf, del_s, del_r, del_rows,
-    in_recv, in_send, att_recv, att_send, ni_recv, ni_send, g_recv, g_send,
+    in_recv, in_send, att_recv, att_send, g_recv, g_send,
     mod_recv, mod_send, del_recv, del_send, db_recv, db_send, loc_sem,
 ):
     peers = lax.axis_size("ctx")
@@ -151,34 +151,26 @@
                 device_id={"ctx": (me + k) % peers}, device_id_type=MESH,
             ).start()
 
-    def send_in(arrays, buf, first):
-        @pl.loop(0, heads)
+    def send_in(arrays, buf, first, start, stop):
+        @pl.loop(start, stop)
         def _(h):
             for a, src in enumerate(arrays):
                 pltpu.make_async_copy(
                     src.at[:, head_cols(me, h)], buf.at[a, h, my_rows, :], in_recv.at[first + a, h]
                 ).start()
 
-            @pl.loop(1, peers)
-            def _(k):
-                t = (me + k) % peers
-                for a, src in enumerate(arrays):
+                @pl.loop(1, peers)
+                def _(k):
+                    t = (me + k) % peers
                     pltpu.make_async_remote_copy(
                         src_ref=src.at[:, head_cols(t, h)], dst_ref=buf.at[a, h, my_rows, :],
                         send_sem=in_send.at[first + a, h], recv_sem=in_recv.at[first + a, h],
                         device_id={"ctx": t}, device_id_type=MESH,
                     ).start()
 
-    send_in((nq, nk, nv), new_buf, 0)
+    send_in((nq, nk, nv), new_buf, 0, 0, heads)
     load_c.start()
     load_o.start()
-    send_in((oq, ok, ov, oc), old_buf, 3)
-    ni_copy = pltpu.make_async_remote_copy(
-        src_ref=ni, dst_ref=ni_out, send_sem=ni_send, recv_sem=ni_recv,
-        device_id={"section": next_section}, device_id_type=MESH,
-    )
-    ni_copy.start()
-
     load_c.wait()
     load_o.wait()
 
@@ -196,6 +188,20 @@
             row[:, c * tokens : (c + 1) * tokens] = flags
             col[c * tokens : (c + 1) * tokens, :] = jnp.broadcast_to(flags, (LANES, tokens)).T
 
+    pltpu.make_async_copy(del_s.at[me], del_r.at[me], del_recv).start()
+
+    @pl.loop(1, peers)
+    def _(k):
+        t = (me + k) % peers
+        pltpu.make_async_remote_copy(
+            src_ref=del_s.at[t], dst_ref=del_r.at[me], send_sem=del_send, recv_sem=del_recv,
+            device_id={"ctx": t}, device_id_type=MESH,
+        ).start()
+
+    send_in((oq, ok, ov, oc), old_buf, 3, 0, heads - 1)
+    send_in((ni,), ni_buf, 7, 0, heads)
+    send_in((oq, ok, ov, oc), old_buf, 3, heads - 1, heads)
+
     def wait_in(buf, a, first, h):
         pltpu.make_async_copy(buf.at[a, h], buf.at[a, h], in_recv.at[first + a, h]).wait()
 
@@ -211,31 +217,31 @@
                 i, bqf, new_buf.at[0, h], new_buf.at[1, h], new_buf.at[2, h], att.at[h], row_n, col_n, limit
             )
 
-        @pl.loop(0, peers)
-        def _(k):
-            t = (me + k) % peers
-            pltpu.make_async_remote_copy(
-                src_ref=att.at[h, token_rows(t), :], dst_ref=att_out.at[:, head_cols(me, h)],
-                send_sem=att_send.at[h], recv_sem=att_recv,
-                device_id={"section": next_section, "ctx": t}, device_id_type=MESH,
-            ).start()
-
-        @pl.when(h == 0)
-        def _():
-            pltpu.make_async_copy(del_s.at[me], del_r.at[me], del_recv).start()
-
-            @pl.loop(1, peers)
-            def _(k):
-                t = (me + k) % peers
-                pltpu.make_async_remote_copy(
-                    src_ref=del_s.at[t], dst_ref=del_r.at[me], send_sem=del_send, recv_sem=del_recv,
-                    device_id={"ctx": t}, device_id_type=MESH,
-                ).start()
-
     pltpu.make_async_copy(del_r, del_r, del_recv).wait()
     for c in range(peers):
         for j in range(heads):
             del_rows[j, :, c * tokens : (c + 1) * tokens] = del_r[c, j : j + 1, :]
+
+    def residual():
+        @pl.loop(0, heads)
+        def _(h):
+            wait_in(ni_buf, 0, 7, h)
+
+            @pl.loop(0, length // bqf)
+            def _(i):
+                rows = pl.ds(pl.multiple_of(i * bqf, bqf), bqf)
+                att[h, rows, :] = (ni_buf[0, h, rows, :].astype(F32) + att[h, rows, :].astype(F32)).astype(BF16)
+
+        @pl.loop(0, heads)
+        def _(h):
+            @pl.loop(0, peers)
+            def _(k):
+                t = (me + k) % peers
+                pltpu.make_async_remote_copy(
+                    src_ref=att.at[h, token_rows(t), :], dst_ref=next_out.at[:, head_cols(me, h)],
+                    send_sem=att_send.at[h], recv_sem=att_recv,
+                    device_id={"section": next_section, "ctx": t}, device_id_type=MESH,
+                ).start()
 
     b_row[...] = jnp.zeros_like(b_row)
     lane = lax.broadcasted_iota(jnp.int32, (8, LANES), 1)
@@ -256,6 +262,10 @@
                 grads.at[0, h], dk_acc, dv_acc, x_scr, ds_scr, b_acc, row_o, col_o, del_rows.at[h], limit,
             )
 
+        @pl.when(h == heads - 2)
+        def _():
+            residual()
+
         grads[1, h] = (dk_acc[...] * width**-0.5).astype(BF16)
         grads[2, h] = dv_acc[...].astype(BF16)
         share = jnp.sum(jnp.sum(b_acc[...], axis=0, keepdims=True), axis=1, keepdims=True)
@@ -263,10 +273,9 @@
         for g, out in enumerate((dq_out, dk_out, dv_out)):
             pltpu.make_async_copy(grads.at[g, h, my_rows, :], out.at[:, head_cols(me, h)], g_recv.at[g]).start()
 
-        @pl.loop(1, peers)
-        def _(k):
-            t = (me + k) % peers
-            for g, out in enumerate((dq_out, dk_out, dv_out)):
+            @pl.loop(1, peers)
+            def _(k):
+                t = (me + k) % peers
                 pltpu.make_async_remote_copy(
                     src_ref=grads.at[g, h, token_rows(t), :], dst_ref=out.at[:, head_cols(me, h)],
                     send_sem=g_send.at[g, h], recv_sem=g_recv.at[g],
@@ -274,6 +283,22 @@
                 ).start()
 
     db_s[...] = b_row[...]
+
+    def drain(ref, sem):
+        pltpu.make_async_copy(ref, ref, sem).wait()
+
+    for j, buf in enumerate((mod_n, mod_o)):
+        drain(buf.at[pl.ds(0, peers - 1)], mod_send.at[j])
+    drain(del_s.at[pl.ds(0, peers - 1)], del_send)
+
+    @pl.loop(0, heads)
+    def _(h):
+        for a in range(3):
+            drain(new_buf.at[a, h, whole, :], in_send.at[a, h])
+        for a in range(4):
+            drain(old_buf.at[a, h, whole, :], in_send.at[3 + a, h])
+        drain(ni_buf.at[0, h, whole, :], in_send.at[7, h])
+
     pltpu.make_async_copy(db_s, db_r.at[replica], db_recv).start()
 
     @pl.loop(1, replicas)
@@ -283,32 +308,19 @@
             device_id={"dp": (replica + k) % replicas}, device_id_type=MESH,
         ).start()
 
+    @pl.loop(0, heads)
+    def _(h):
+        drain(att.at[h], att_send.at[h])
+        for g in range(3):
+            drain(grads.at[g, h, whole, :], g_send.at[g, h])
+
     pltpu.make_async_copy(db_r, db_r, db_recv).wait()
     acc = db_r[0]
     for r in range(1, replicas):
         acc = acc + db_r[r]
     db_out[...] = acc
-
-    def drain(ref, sem):
-        pltpu.make_async_copy(ref, ref, sem).wait()
-
-    for j, buf in enumerate((mod_n, mod_o)):
-        drain(buf.at[pl.ds(0, peers - 1)], mod_send.at[j])
-    drain(del_s.at[pl.ds(0, peers - 1)], del_send)
     drain(db_r.at[pl.ds(0, replicas - 1)], db_send)
-
-    @pl.loop(0, heads)
-    def _(h):
-        for a in range(3):
-            drain(new_buf.at[a, h, whole, :], in_send.at[a, h])
-        for a in range(4):
-            drain(old_buf.at[a, h, whole, :], in_send.at[3 + a, h])
-        drain(att.at[h], att_send.at[h])
-        for g in range(3):
-            drain(grads.at[g, h, whole, :], g_send.at[g, h])
-
-    ni_copy.wait()
-    drain(att_out, att_recv)
+    drain(next_out, att_recv)
     for g, out in enumerate((dq_out, dk_out, dv_out)):
         drain(out, g_recv.at[g])
 
@@ -331,14 +343,15 @@
     full = jax.ShapeDtypeStruct((tokens, features), BF16)
     dma = pltpu.SemaphoreType.DMA
     any_spec = pl.BlockSpec(memory_space=pl.ANY)
-    att, shifted, dq, dk, dv, db = pl.pallas_call(
+    following, dq, dk, dv, db = pl.pallas_call(
         functools.partial(body, heads, bqf, bq, bk),
-        out_shape=[full] * 5 + [jax.ShapeDtypeStruct((8, LANES), F32)],
+        out_shape=[full] * 4 + [jax.ShapeDtypeStruct((8, LANES), F32)],
         in_specs=[any_spec] * 11 + [pl.BlockSpec(memory_space=pltpu.SMEM)],
-        out_specs=[any_spec] * 5 + [pl.BlockSpec(memory_space=pltpu.VMEM)],
+        out_specs=[any_spec] * 4 + [pl.BlockSpec(memory_space=pltpu.VMEM)],
         scratch_shapes=[
             pltpu.VMEM((3, heads, length, width), BF16),
             pltpu.VMEM((4, heads, length, width), BF16),
+            pltpu.VMEM((1, heads, length, width), BF16),
             pltpu.VMEM((heads, length, width), BF16),
             pltpu.VMEM((3, heads, length, width), BF16),
             pltpu.VMEM((length, width), F32),
@@ -360,9 +373,8 @@
             pltpu.VMEM((peers, 8, tokens), F32),
             pltpu.VMEM((peers, 8, tokens), F32),
             pltpu.VMEM((heads, 1, length), F32),
-            dma((7, heads)), dma((7, heads)),
+            dma((8, heads)), dma((8, heads)),
             dma, dma((heads,)),
-            dma, dma,
             dma((3,)), dma((3, heads)),
             dma((2,)), dma((2,)),
             dma, dma,
@@ -377,12 +389,11 @@
         flat(old_query), flat(old_key), flat(old_value), flat(old_output), flat(old_cotangent),
         new_modality.reshape(1, tokens), old_modality.reshape(1, tokens), cross_bias,
     )
-    summed = (shifted.astype(F32) + att.astype(F32)).astype(BF16)
 
     def whole(x):
         return x[None, None]
 
-    return whole(summed), whole(dq), whole(dk), whole(dv), db[:1, :heads]
+    return whole(following), whole(dq), whole(dk), whole(dv), db[:1, :heads]
 
 
 def solution(mesh):

time: 286 us -> 235 us (0.82)
  Pallas kernels: 275 us -> 225 us
  other arithmetic: 3.52 us -> 0 us
    pallas_call x1, Pallas kernels: 275 us -> 225 us  [shards(): pl.pallas_call(functools.partial(body, heads, bqf, bq, bk), out_shape=[fu...]
    broadcast_in_dim x1 -> x0, other arithmetic: 3.52 us -> none  [whole(): return x[None, None]]
    unnamed x9 -> x10, local copies, waits for them, and re-layouts: 5.1 us -> 7.9 us
where the time goes in v2:
time: 235 us
  Pallas kernels  225 us (96%)
  local copies, waits for them, and re-layouts  9.1 us (4%)
    pallas_call x1, Pallas kernels, shards(): pl.pallas_call(functools.partial(body, heads, bqf, bq, bk), out_shape=[fu...  225 us
    unnamed x10, local copies, waits for them, and re-layouts  7.9 us

profile of v2, /device:TPU:1, one launch (start us, length us, event | category | flops | bytes accessed | tf_op | source)
XLA Modules:
  0.0 235.0 jit_solution(17837740327116843058)
XLA Ops:
  0.6 225.3 %shard_map.155 = (bf16[128,6144]{1,0:T(8,128)(2,1)}, bf16[128,6144]{1,0:T(8,128)(2,1)}, bf16[128,6144]{1,0:T(8,128)(2,1)}, bf16[128,6144]{1,0:T(8,128)(2,1)}, f32[8,128]{1,0:T(8,128)}) custom-call(bf16[128,6144]{1,0:T(8,128)(2,1)} %bitcast.19, bf16[128,6144]{1,0:T(8,128)(2,1)} %bitcast.20, bf16[128,6144]{1,0:T(8,128)(2,1)} %bitcast.21, ...), custom_call_target="tpu_custom_call" | custom-call | tf_op jit(solution)/shard_map/pallas_call | solution.py:346
  225.9 1.2 slice.3
  227.1 0.0 copy-start.2
  227.1 2.8 %copy.21 = bf16[1,1,128,6144]{3,2,1,0:T(8,128)(2,1)} copy(bf16[1,1,128,6144]{3,2,1,0:T(8,128)(2,1)} %bitcast.18) | data formatting | bytes 3145728
  229.9 0.0 copy-done.2
  229.9 0.0 copy-start.1
  229.9 1.1 copy.22
  231.1 0.8 copy-done.1
  231.9 0.0 copy-start
  231.9 1.1 copy.23
  233.0 0.8 copy-done
  233.9 1.1 copy.24
Async XLA Ops:
  227.1 2.8 %copy-start.2 = (bf16[128,6144]{1,0:T(8,128)(2,1)S(1)}, bf16[128,6144]{1,0:T(8,128)(2,1)}, u32[]{:S(2)}) copy-start(bf16[128,6144]{1,0:T(8,128)(2,1)} %get-tuple-element.11) | copy-start | bytes 4718596
  229.9 2.0 copy-start.1
  231.9 2.0 copy-start

commit v3 on v2

--- a/solution.py
+++ b/solution.py
@@ -198,9 +198,9 @@
             device_id={"ctx": t}, device_id_type=MESH,
         ).start()
 
-    send_in((oq, ok, ov, oc), old_buf, 3, 0, heads - 1)
+    send_in((oq, ok, ov, oc), old_buf, 3, 0, 1)
     send_in((ni,), ni_buf, 7, 0, heads)
-    send_in((oq, ok, ov, oc), old_buf, 3, heads - 1, heads)
+    send_in((oq, ok, ov, oc), old_buf, 3, 1, heads)
 
     def wait_in(buf, a, first, h):
         pltpu.make_async_copy(buf.at[a, h], buf.at[a, h], in_recv.at[first + a, h]).wait()
@@ -222,26 +222,20 @@
         for j in range(heads):
             del_rows[j, :, c * tokens : (c + 1) * tokens] = del_r[c, j : j + 1, :]
 
-    def residual():
-        @pl.loop(0, heads)
-        def _(h):
-            wait_in(ni_buf, 0, 7, h)
-
-            @pl.loop(0, length // bqf)
-            def _(i):
-                rows = pl.ds(pl.multiple_of(i * bqf, bqf), bqf)
-                att[h, rows, :] = (ni_buf[0, h, rows, :].astype(F32) + att[h, rows, :].astype(F32)).astype(BF16)
-
-        @pl.loop(0, heads)
-        def _(h):
-            @pl.loop(0, peers)
-            def _(k):
-                t = (me + k) % peers
-                pltpu.make_async_remote_copy(
-                    src_ref=att.at[h, token_rows(t), :], dst_ref=next_out.at[:, head_cols(me, h)],
-                    send_sem=att_send.at[h], recv_sem=att_recv,
-                    device_id={"section": next_section, "ctx": t}, device_id_type=MESH,
-                ).start()
+    def residual(h):
+        wait_in(ni_buf, 0, 7, h)
+
+        @pl.loop(0, length // bqf)
+        def _(i):
+            rows = pl.ds(pl.multiple_of(i * bqf, bqf), bqf)
+            att[h, rows, :] = (ni_buf[0, h, rows, :].astype(F32) + att[h, rows, :].astype(F32)).astype(BF16)
+
+    def send_next(h, t):
+        pltpu.make_async_remote_copy(
+            src_ref=att.at[h, token_rows(t), :], dst_ref=next_out.at[:, head_cols(me, h)],
+            send_sem=att_send.at[h], recv_sem=att_recv,
+            device_id={"section": next_section, "ctx": t}, device_id_type=MESH,
+        ).start()
 
     b_row[...] = jnp.zeros_like(b_row)
     lane = lax.broadcasted_iota(jnp.int32, (8, LANES), 1)
@@ -262,10 +256,7 @@
                 grads.at[0, h], dk_acc, dv_acc, x_scr, ds_scr, b_acc, row_o, col_o, del_rows.at[h], limit,
             )
 
-        @pl.when(h == heads - 2)
-        def _():
-            residual()
-
+        residual(h)
         grads[1, h] = (dk_acc[...] * width**-0.5).astype(BF16)
         grads[2, h] = dv_acc[...].astype(BF16)
         share = jnp.sum(jnp.sum(b_acc[...], axis=0, keepdims=True), axis=1, keepdims=True)
@@ -281,6 +272,11 @@
                     send_sem=g_send.at[g, h], recv_sem=g_recv.at[g],
                     device_id={"ctx": t}, device_id_type=MESH,
                 ).start()
+                if g == 0:
+                    send_next(h, (me + k + peers // 2) % peers)
+
+            if g == 0:
+                send_next(h, (me + peers // 2) % peers)
 
     db_s[...] = b_row[...]
 
@@ -323,6 +319,24 @@
     drain(next_out, att_recv)
     for g, out in enumerate((dq_out, dk_out, dv_out)):
         drain(out, g_recv.at[g])
+
+
+def hand_over(heads, chunks, *refs):
+    count = (len(refs) - 3) // 2
+    sources, db, targets, db_out = refs[:count], refs[count], refs[count + 1 : 2 * count + 1], refs[2 * count + 1]
+    (sem,) = refs[2 * count + 2 :]
+    step = sources[0].shape[0] // chunks
+
+    def store(a, c):
+        rows = pl.ds(c * step, step)
+        return pltpu.make_async_copy(sources[a].at[rows, :], targets[a].at[rows, :], sem.at[a, c])
+
+    pieces = [(a, c) for a in range(count) for c in range(chunks)]
+    for piece in pieces:
+        store(*piece).start()
+    db_out[...] = db[:1, :heads]
+    for piece in pieces:
+        store(*piece).wait()
 
 
 def shards(
@@ -342,12 +356,13 @@
 
     full = jax.ShapeDtypeStruct((tokens, features), BF16)
     dma = pltpu.SemaphoreType.DMA
-    any_spec = pl.BlockSpec(memory_space=pl.ANY)
+    hbm_spec = pl.BlockSpec(memory_space=pltpu.HBM)
+    vmem_spec = pl.BlockSpec(memory_space=pltpu.VMEM)
     following, dq, dk, dv, db = pl.pallas_call(
         functools.partial(body, heads, bqf, bq, bk),
-        out_shape=[full] * 4 + [jax.ShapeDtypeStruct((8, LANES), F32)],
-        in_specs=[any_spec] * 11 + [pl.BlockSpec(memory_space=pltpu.SMEM)],
-        out_specs=[any_spec] * 4 + [pl.BlockSpec(memory_space=pltpu.VMEM)],
+        out_shape=[pltpu.VMEM((tokens, features), BF16)] * 4 + [pltpu.VMEM((8, LANES), F32)],
+        in_specs=[hbm_spec] * 11 + [pl.BlockSpec(memory_space=pltpu.SMEM)],
+        out_specs=[vmem_spec] * 5,
         scratch_shapes=[
             pltpu.VMEM((3, heads, length, width), BF16),
             pltpu.VMEM((4, heads, length, width), BF16),
@@ -382,7 +397,7 @@
             dma((2,)),
         ],
         compiler_params=pltpu.CompilerParams(
-            collective_id=0, has_side_effects=True, vmem_limit_bytes=62 << 20
+            collective_id=0, has_side_effects=True, vmem_limit_bytes=57 << 20
         ),
     )(
         flat(new_input), flat(new_query), flat(new_key), flat(new_value),
@@ -390,10 +405,20 @@
         new_modality.reshape(1, tokens), old_modality.reshape(1, tokens), cross_bias,
     )
 
+    chunks = 4
+    following, dq, dk, dv, db = pl.pallas_call(
+        functools.partial(hand_over, heads, chunks),
+        out_shape=[full] * 4 + [jax.ShapeDtypeStruct((1, heads), F32)],
+        in_specs=[vmem_spec] * 5,
+        out_specs=[hbm_spec] * 4 + [vmem_spec],
+        scratch_shapes=[dma((4, chunks))],
+        compiler_params=pltpu.CompilerParams(vmem_limit_bytes=30 << 20),
+    )(following, dq, dk, dv, db)
+
     def whole(x):
         return x[None, None]
 
-    return whole(following), whole(dq), whole(dk), whole(dv), db[:1, :heads]
+    return whole(following), whole(dq), whole(dk), whole(dv), db
 
 
 def solution(mesh):

time: 235 us -> 222 us (0.945)
  local copies, waits for them, and re-layouts: 9.1 us -> 0 us
  Pallas kernels: 225 us -> 221 us
    unnamed x10 -> x0, local copies, waits for them, and re-layouts: 7.9 us -> none
    pallas_call x1 -> x2, Pallas kernels: 225 us -> 221 us  [the longest x1 218 us: shards(): pl.pallas_call(functools.partial(body, heads, bqf, bq, bk), out_shape=[pl...]
where the time goes in v3:
time: 222 us
  Pallas kernels  221 us (100%)
    pallas_call x1, Pallas kernels, shards(): pl.pallas_call(functools.partial(body, heads, bqf, bq, bk), out_shape=[pl...  218 us

profile of v3, /device:TPU:1, one launch (start us, length us, event | category | flops | bytes accessed | tf_op | source)
XLA Modules:
  0.0 221.6 jit_solution(12509220831659409847)
XLA Ops:
  0.6 217.6 %shard_map.155 = (bf16[128,6144]{1,0:T(8,128)(2,1)S(1)}, bf16[128,6144]{1,0:T(8,128)(2,1)S(1)}, bf16[128,6144]{1,0:T(8,128)(2,1)S(1)}, bf16[128,6144]{1,0:T(8,128)(2,1)S(1)}, f32[8,128]{1,0:T(8,128)S(1)}) custom-call(bf16[128,6144]{1,0:T(8,128)(2,1)} %bitcast.15, bf16[128,6144]{1,0:T(8,128)(2,1)} %bitcast.16, bf16[128,6144]{1,0:T(8,128)(2,1)} %bitcast.17, ...), custom_call_target="tpu_custom_call" | custom-call | tf_op jit(solution)/shard_map/pallas_call | solution.py:361
  218.3 3.3 %shard_map.156 = (bf16[128,6144]{1,0:T(8,128)(2,1)}, bf16[128,6144]{1,0:T(8,128)(2,1)}, bf16[128,6144]{1,0:T(8,128)(2,1)}, bf16[128,6144]{1,0:T(8,128)(2,1)}, f32[1,3]{1,0:T(1,128)}) custom-call(bf16[128,6144]{1,0:T(8,128)(2,1)S(1)} %get-tuple-element.15.refs_0_, bf16[128,6144]{1,0:T(8,128)(2,1)S(1)} %get-tuple-element.16.refs_1_, ...), custom_call_target="tpu_custom_call" | custom-call | tf_op jit(solution)/shard_map/pallas_call | solution.py:409

commit v4 on v3

--- a/solution.py
+++ b/solution.py
@@ -198,9 +198,9 @@
             device_id={"ctx": t}, device_id_type=MESH,
         ).start()
 
-    send_in((oq, ok, ov, oc), old_buf, 3, 0, 1)
-    send_in((ni,), ni_buf, 7, 0, heads)
-    send_in((oq, ok, ov, oc), old_buf, 3, 1, heads)
+    for h in range(heads):
+        send_in((oq, ok, ov, oc), old_buf, 3, h, h + 1)
+        send_in((ni,), ni_buf, 7, h, h + 1)
 
     def wait_in(buf, a, first, h):
         pltpu.make_async_copy(buf.at[a, h], buf.at[a, h], in_recv.at[first + a, h]).wait()
@@ -272,7 +272,9 @@
                     send_sem=g_send.at[g, h], recv_sem=g_recv.at[g],
                     device_id={"ctx": t}, device_id_type=MESH,
                 ).start()
-                if g == 0:
+
+                @pl.when(k % 3 == g)
+                def _():
                     send_next(h, (me + k + peers // 2) % peers)
 
             if g == 0:

time: 222 us -> 220 us (level)
  no operation moved by 1% of the time
where the time goes in v4:
time: 220 us
  Pallas kernels  219 us (100%)
    pallas_call x1, Pallas kernels, shards(): pl.pallas_call(functools.partial(body, heads, bqf, bq, bk), out_shape=[pl...  216 us

profile of v4, /device:TPU:1, one launch (start us, length us, event | category | flops | bytes accessed | tf_op | source)
XLA Modules:
  0.0 219.5 jit_solution(7042748588756952687)
XLA Ops:
  0.6 215.6 %shard_map.155 = (bf16[128,6144]{1,0:T(8,128)(2,1)S(1)}, bf16[128,6144]{1,0:T(8,128)(2,1)S(1)}, bf16[128,6144]{1,0:T(8,128)(2,1)S(1)}, bf16[128,6144]{1,0:T(8,128)(2,1)S(1)}, f32[8,128]{1,0:T(8,128)S(1)}) custom-call(bf16[128,6144]{1,0:T(8,128)(2,1)} %bitcast.15, bf16[128,6144]{1,0:T(8,128)(2,1)} %bitcast.16, bf16[128,6144]{1,0:T(8,128)(2,1)} %bitcast.17, ...), custom_call_target="tpu_custom_call" | custom-call | tf_op jit(solution)/shard_map/pallas_call | solution.py:363
  216.2 3.3 %shard_map.156 = (bf16[128,6144]{1,0:T(8,128)(2,1)}, bf16[128,6144]{1,0:T(8,128)(2,1)}, bf16[128,6144]{1,0:T(8,128)(2,1)}, bf16[128,6144]{1,0:T(8,128)(2,1)}, f32[1,3]{1,0:T(1,128)}) custom-call(bf16[128,6144]{1,0:T(8,128)(2,1)S(1)} %get-tuple-element.15.refs_0_, bf16[128,6144]{1,0:T(8,128)(2,1)S(1)} %get-tuple-element.16.refs_1_, ...), custom_call_target="tpu_custom_call" | custom-call | tf_op jit(solution)/shard_map/pallas_call | solution.py:411
